TPU v7x, 128 devices: a whole 4x4x4 slice. The times are simulated.
128 devices in a mesh: dp: 4 (over x), seq: 8 (over z, core), tensor: 4 (over y).
Axes of the slice: x: 4, y: 4, z: 4, core: 2. Of those that a mesh axis runs over, the one named last changes fastest.
Arguments:
- block_input: bfloat16 [2048, 4, 1024], P('seq', 'dp', 'tensor'), may hold values from -6 to 6
- attn_gain: bfloat16 [1024], P(('dp', 'seq')), may hold values from 0.099609375 to 1.8984375
- ffn_gain: bfloat16 [1024], P(('dp', 'seq')), may hold values from 0.099609375 to 1.8984375
- query_gain: bfloat16 [64], replicated, may hold values from 0.5 to 2.5
- key_gain: bfloat16 [64], replicated, may hold values from 0.5 to 2.5
- query_weight: bfloat16 [1024, 1024], P(('dp', 'seq'), 'tensor'), may hold values from -0.1875 to 0.1875
- key_weight: bfloat16 [1024, 512], P(('dp', 'seq'), 'tensor'), may hold values from -0.1875 to 0.1875
- value_weight: bfloat16 [1024, 512], P(('dp', 'seq'), 'tensor'), may hold values from -0.1875 to 0.1875
- out_weight: bfloat16 [1024, 1024], P(('dp', 'seq'), 'tensor'), may hold values from -2 to 2
- gate_weight: bfloat16 [1024, 4608], P(('dp', 'seq'), 'tensor'), may hold values from -0.1875 to 0.1875
- up_weight: bfloat16 [1024, 4608], P(('dp', 'seq'), 'tensor'), may hold values from -0.1875 to 0.1875
- down_weight: bfloat16 [1024, 4608], P(('dp', 'seq'), 'tensor'), may hold values from -0.09375 to 0.09375
- cotangent: bfloat16 [2048, 4, 1024], P('seq', 'dp', 'tensor'), may hold values from -6 to 6
Outputs:
- block_output: bfloat16 [2048, 4, 1024], P('seq', 'dp', 'tensor')
- input_grad: bfloat16 [2048, 4, 1024], P('seq', 'dp', 'tensor')
- attn_gain_grad: float32 [1024], P(('dp', 'seq'))
- ffn_gain_grad: float32 [1024], P(('dp', 'seq'))
- query_gain_grad: float32 [64], replicated
- key_gain_grad: float32 [64], replicated
- query_grad: float32 [1024, 1024], P(('dp', 'seq'), 'tensor')
- key_grad: float32 [1024, 512], P(('dp', 'seq'), 'tensor')
- value_grad: float32 [1024, 512], P(('dp', 'seq'), 'tensor')
- out_grad: float32 [1024, 1024], P(('dp', 'seq'), 'tensor')
- gate_grad: float32 [1024, 4608], P(('dp', 'seq'), 'tensor')
- up_grad: float32 [1024, 4608], P(('dp', 'seq'), 'tensor')
- down_grad: float32 [1024, 4608], P(('dp', 'seq'), 'tensor')
All inputs are finite; a program needn't handle non-finite values.
Results may differ from a plain program's by a relative error of at most 0.03.
Values may be sent and summed in bfloat16 or wider, within the bound.
No kernel may reach another device: no remote copies, remote signals or barrier semaphores. Data moves between devices by JAX's collectives and lax.ppermute only.
A program may use at most 64 MiB of HBM per device.

v0:
```python
import jax
import jax.numpy as jnp
from jax import lax
from jax.sharding import PartitionSpec as P

HD = 64
epsilon = 1e-05
rope_base = 1000000.0
far_below = -1e30


def rms_scale(values, gain):
    return values * lax.rsqrt(jnp.mean(values * values, axis=-1, keepdims=True) + epsilon) * gain


def swiglu(gate, up_part):
    return jax.nn.silu(gate) * up_part


def rotate(values, cosine, sine):
    half = values.shape[-1] // 2
    first = values[..., :half]
    second = values[..., half:]
    return jnp.concatenate(
        [first * cosine - second * sine, second * cosine + first * sine], axis=-1
    )


def project(left, right):
    return jnp.dot(left, right, preferred_element_type=jnp.float32)


def contract_rows(left, right):
    return lax.dot_general(
        left, right, (((0,), (0,)), ((), ())), preferred_element_type=jnp.float32
    )


def contract_cols(left, right):
    return lax.dot_general(
        left, right, (((1,), (1,)), ((), ())), preferred_element_type=jnp.float32
    )


def body(
    block_input,
    attn_gain,
    ffn_gain,
    query_gain,
    key_gain,
    query_weight,
    key_weight,
    value_weight,
    out_weight,
    gate_weight,
    up_weight,
    down_weight,
    cotangent,
):
    local_full = lax.all_gather(block_input, "tensor", axis=2, tiled=True)
    span, seq_local, width = local_full.shape
    row_count = span * seq_local
    feature_part = block_input.shape[2]
    feature_start = lax.axis_index("tensor") * feature_part
    seq_devices = lax.axis_size("seq")
    my_first = lax.axis_index("seq") * span
    kv_heads = key_weight.shape[1] // HD
    group = query_weight.shape[1] // key_weight.shape[1]
    kv_width = kv_heads * HD
    score_scale = HD ** (-0.5)
    gathered = (
        lax.all_gather(query_weight, ("dp", "seq"), axis=0, tiled=True),
        lax.all_gather(key_weight, ("dp", "seq"), axis=0, tiled=True),
        lax.all_gather(value_weight, ("dp", "seq"), axis=0, tiled=True),
        lax.all_gather(out_weight, ("dp", "seq"), axis=0, tiled=True),
        lax.all_gather(gate_weight, ("dp", "seq"), axis=0, tiled=True),
        lax.all_gather(up_weight, ("dp", "seq"), axis=0, tiled=True),
        lax.all_gather(down_weight, ("dp", "seq"), axis=0, tiled=True),
        lax.all_gather(attn_gain, ("dp", "seq"), axis=0, tiled=True),
        lax.all_gather(ffn_gain, ("dp", "seq"), axis=0, tiled=True),
    )
    (
        query_full,
        key_full,
        value_full,
        out_full,
        gate_full,
        up_full,
        down_full,
        gain_attn,
        gain_ffn,
    ) = gathered
    gain_one = gain_attn.astype(jnp.float32)
    gain_two = gain_ffn.astype(jnp.float32)
    head_query = query_gain.astype(jnp.float32)
    head_key = key_gain.astype(jnp.float32)
    positions = my_first + jnp.arange(span, dtype=jnp.int32)
    frequency = jnp.power(rope_base, -2.0 * jnp.arange(HD // 2, dtype=jnp.float32) / HD)
    angle = positions.astype(jnp.float32)[:, None] * frequency[None, :]
    cosine = jnp.cos(angle)[:, None, None, :]
    sine = jnp.sin(angle)[:, None, None, :]

    def shape_heads(raw, gain):
        heads = raw.reshape(span, seq_local, raw.shape[1] // HD, HD)
        return rotate(rms_scale(heads, gain), cosine, sine)

    base = local_full.reshape(row_count, width).astype(jnp.float32)
    normed_one = rms_scale(base, gain_one).astype(jnp.bfloat16)
    query_raw = project(normed_one, query_full)
    key_raw = project(normed_one, key_full)
    value_raw = project(normed_one, value_full)
    query_rot, pull_query = jax.vjp(shape_heads, query_raw, head_query)
    key_rot, pull_key = jax.vjp(shape_heads, key_raw, head_key)
    query_b = query_rot.astype(jnp.bfloat16).reshape(span, seq_local, kv_heads, group, HD)
    key_b = key_rot.astype(jnp.bfloat16).reshape(span, seq_local, kv_width)
    value_b = value_raw.astype(jnp.bfloat16).reshape(span, seq_local, kv_width)
    packed = jnp.concatenate([key_b, value_b], axis=-1)

    def split_piece(piece):
        count = piece.shape[0]
        return (
            piece[..., :kv_width].reshape(count, seq_local, kv_heads, HD),
            piece[..., kv_width:].reshape(count, seq_local, kv_heads, HD),
        )

    def scores_for(piece_keys):
        raw = (
            jnp.einsum("cskgd,pskd->cskgp", query_b, piece_keys, preferred_element_type=jnp.float32)
            * score_scale
        )
        key_pos = jnp.arange(piece_keys.shape[0], dtype=jnp.int32)
        allowed = (positions[:, None] >= key_pos[None, :])[:, None, None, None, :]
        return (raw, allowed)

    stat_shape = (span, seq_local, kv_heads, group)
    initial = (
        jnp.full(stat_shape, far_below, jnp.float32),
        jnp.zeros(stat_shape, jnp.float32),
        jnp.zeros(stat_shape + (HD,), jnp.float32),
    )
    piece = lax.all_gather(packed, "seq", axis=0, tiled=True)

    def forward_work(state):
        top, total, accum = state
        piece_keys, piece_values = split_piece(piece)
        raw, allowed = scores_for(piece_keys)
        new_top = jnp.maximum(top, jnp.max(jnp.where(allowed, raw, far_below), axis=-1))
        expo = jnp.where(allowed, jnp.exp(raw - new_top[..., None]), 0.0)
        total = jnp.sum(expo, axis=-1)
        accum = jnp.einsum(
            "cskgp,pskd->cskgd",
            expo.astype(jnp.bfloat16),
            piece_values,
            preferred_element_type=jnp.float32,
        )
        return (new_top, total, accum)

    top, total, accum = lax.cond(
        jnp.int32(0) <= my_first + span - 1, forward_work, lambda state: state, initial
    )
    attn_values = accum / total[..., None]
    log_total = top + jnp.log(total)
    attn_b = attn_values.reshape(row_count, -1).astype(jnp.bfloat16)
    attn_sum = lax.psum(contract_cols(attn_b, out_full).astype(jnp.bfloat16), "tensor").astype(
        jnp.float32
    )
    middle = base + attn_sum
    normed_two = rms_scale(middle, gain_two).astype(jnp.bfloat16)
    gate = project(normed_two, gate_full)
    up_part = project(normed_two, up_full)
    hidden = swiglu(gate, up_part).astype(jnp.bfloat16)
    ffn_mine = lax.psum_scatter(
        contract_cols(hidden, down_full).reshape(span, seq_local, width).astype(jnp.bfloat16),
        "tensor",
        scatter_dimension=2,
        tiled=True,
    ).astype(jnp.float32)
    middle_mine = lax.dynamic_slice_in_dim(
        middle.reshape(span, seq_local, width), feature_start, feature_part, 2
    )
    block_output = (middle_mine + ffn_mine).astype(jnp.bfloat16)
    again = (
        lax.all_gather(query_weight, ("dp", "seq"), axis=0, tiled=True),
        lax.all_gather(key_weight, ("dp", "seq"), axis=0, tiled=True),
        lax.all_gather(value_weight, ("dp", "seq"), axis=0, tiled=True),
        lax.all_gather(out_weight, ("dp", "seq"), axis=0, tiled=True),
        lax.all_gather(gate_weight, ("dp", "seq"), axis=0, tiled=True),
        lax.all_gather(up_weight, ("dp", "seq"), axis=0, tiled=True),
        lax.all_gather(down_weight, ("dp", "seq"), axis=0, tiled=True),
    )
    query_back, key_back, value_back, out_back, gate_back, up_back, down_back = again
    cot_full = lax.all_gather(cotangent, "tensor", axis=2, tiled=True).reshape(row_count, width)
    hidden_grad = project(cot_full, down_back)
    down_sum = contract_rows(cot_full, hidden)
    _, pull_swiglu = jax.vjp(swiglu, gate, up_part)
    gate_grad, up_grad = pull_swiglu(hidden_grad)
    gate_gb = gate_grad.astype(jnp.bfloat16)
    up_gb = up_grad.astype(jnp.bfloat16)
    normed_two_grad = lax.psum(
        (contract_cols(gate_gb, gate_back) + contract_cols(up_gb, up_back)).astype(jnp.bfloat16),
        "tensor",
    ).astype(jnp.float32)
    gate_sum = contract_rows(normed_two, gate_gb)
    up_sum = contract_rows(normed_two, up_gb)
    _, pull_two = jax.vjp(rms_scale, middle, gain_two)
    middle_norm_grad, gain_two_grad = pull_two(normed_two_grad)
    middle_grad = cot_full.astype(jnp.float32) + middle_norm_grad
    middle_gb = middle_grad.astype(jnp.bfloat16)
    attn_grad = project(middle_gb, out_back)
    out_sum = contract_rows(middle_gb, attn_b)
    attn_full = attn_grad.reshape(span, seq_local, kv_heads, group, HD)
    attn_gb = attn_full.astype(jnp.bfloat16)
    delta = jnp.sum(attn_full * attn_values, axis=-1)
    full_length = span * seq_devices
    back_initial = (
        jnp.zeros(stat_shape + (HD,), jnp.float32),
        jnp.zeros((full_length, seq_local, 2 * kv_width), jnp.float32),
    )
    backward_piece = lax.all_gather(packed, "seq", axis=0, tiled=True)

    def backward_work(state):
        piece_keys, piece_values = split_piece(backward_piece)
        raw, allowed = scores_for(piece_keys)
        probs = jnp.where(allowed, jnp.exp(raw - log_total[..., None]), 0.0)
        prob_grad = jnp.einsum(
            "cskgd,pskd->cskgp", attn_gb, piece_values, preferred_element_type=jnp.float32
        )
        score_gb = (probs * (prob_grad - delta[..., None])).astype(jnp.bfloat16)
        query_acc = (
            jnp.einsum(
                "cskgp,pskd->cskgd", score_gb, piece_keys, preferred_element_type=jnp.float32
            )
            * score_scale
        )
        key_part = (
            jnp.einsum("cskgp,cskgd->pskd", score_gb, query_b, preferred_element_type=jnp.float32)
            * score_scale
        )
        value_part = jnp.einsum(
            "cskgp,cskgd->pskd",
            probs.astype(jnp.bfloat16),
            attn_gb,
            preferred_element_type=jnp.float32,
        )
        count = backward_piece.shape[0]
        term = jnp.concatenate(
            [
                key_part.reshape(count, seq_local, kv_width),
                value_part.reshape(count, seq_local, kv_width),
            ],
            axis=-1,
        )
        return (query_acc, term)

    query_hgrad, kv_total = lax.cond(
        jnp.int32(0) <= my_first + span - 1, backward_work, lambda state: state, back_initial
    )
    kv_mine = lax.psum_scatter(
        kv_total.astype(jnp.bfloat16), "seq", scatter_dimension=0, tiled=True
    ).astype(jnp.float32)
    query_raw_grad, query_gain_part = pull_query(
        query_hgrad.reshape(span, seq_local, kv_heads * group, HD)
    )
    key_raw_grad, key_gain_part = pull_key(
        kv_mine[..., :kv_width].reshape(span, seq_local, kv_heads, HD)
    )
    query_gb = query_raw_grad.astype(jnp.bfloat16)
    key_gb = key_raw_grad.astype(jnp.bfloat16)
    value_gb = kv_mine[..., kv_width:].reshape(row_count, kv_width).astype(jnp.bfloat16)
    normed_one_grad = lax.psum(
        (
            contract_cols(query_gb, query_back)
            + contract_cols(key_gb, key_back)
            + contract_cols(value_gb, value_back)
        ).astype(jnp.bfloat16),
        "tensor",
    ).astype(jnp.float32)
    query_sum = contract_rows(normed_one, query_gb)
    key_sum = contract_rows(normed_one, key_gb)
    value_sum = contract_rows(normed_one, value_gb)
    _, pull_one = jax.vjp(rms_scale, base, gain_one)
    base_norm_grad, gain_one_grad = pull_one(normed_one_grad)
    input_full = (middle_grad + base_norm_grad).reshape(span, seq_local, width)
    input_grad = lax.dynamic_slice_in_dim(input_full, feature_start, feature_part, 2).astype(
        jnp.bfloat16
    )
    summed = (
        lax.psum_scatter(
            gain_one_grad.astype(jnp.bfloat16), ("dp", "seq"), scatter_dimension=0, tiled=True
        ).astype(jnp.float32),
        lax.psum_scatter(
            gain_two_grad.astype(jnp.bfloat16), ("dp", "seq"), scatter_dimension=0, tiled=True
        ).astype(jnp.float32),
        lax.psum_scatter(
            query_sum.astype(jnp.bfloat16), ("dp", "seq"), scatter_dimension=0, tiled=True
        ).astype(jnp.float32),
        lax.psum_scatter(
            key_sum.astype(jnp.bfloat16), ("dp", "seq"), scatter_dimension=0, tiled=True
        ).astype(jnp.float32),
        lax.psum_scatter(
            value_sum.astype(jnp.bfloat16), ("dp", "seq"), scatter_dimension=0, tiled=True
        ).astype(jnp.float32),
        lax.psum_scatter(
            out_sum.astype(jnp.bfloat16), ("dp", "seq"), scatter_dimension=0, tiled=True
        ).astype(jnp.float32),
        lax.psum_scatter(
            gate_sum.astype(jnp.bfloat16), ("dp", "seq"), scatter_dimension=0, tiled=True
        ).astype(jnp.float32),
        lax.psum_scatter(
            up_sum.astype(jnp.bfloat16), ("dp", "seq"), scatter_dimension=0, tiled=True
        ).astype(jnp.float32),
        lax.psum_scatter(
            down_sum.astype(jnp.bfloat16), ("dp", "seq"), scatter_dimension=0, tiled=True
        ).astype(jnp.float32),
    )
    head_sums = lax.psum((query_gain_part, key_gain_part), ("dp", "seq", "tensor"))
    return (
        block_output,
        input_grad,
        summed[0],
        summed[1],
        head_sums[0],
        head_sums[1],
        summed[2],
        summed[3],
        summed[4],
        summed[5],
        summed[6],
        summed[7],
        summed[8],
    )


def solution(mesh):
    return jax.shard_map(
        body,
        mesh=mesh,
        in_specs=(
            P("seq", "dp", "tensor"),
            P(("dp", "seq")),
            P(("dp", "seq")),
            P(),
            P(),
            P(("dp", "seq"), "tensor"),
            P(("dp", "seq"), "tensor"),
            P(("dp", "seq"), "tensor"),
            P(("dp", "seq"), "tensor"),
            P(("dp", "seq"), "tensor"),
            P(("dp", "seq"), "tensor"),
            P(("dp", "seq"), "tensor"),
            P("seq", "dp", "tensor"),
        ),
        out_specs=(
            P("seq", "dp", "tensor"),
            P("seq", "dp", "tensor"),
            P(("dp", "seq")),
            P(("dp", "seq")),
            P(),
            P(),
            P(("dp", "seq"), "tensor"),
            P(("dp", "seq"), "tensor"),
            P(("dp", "seq"), "tensor"),
            P(("dp", "seq"), "tensor"),
            P(("dp", "seq"), "tensor"),
            P(("dp", "seq"), "tensor"),
            P(("dp", "seq"), "tensor"),
        ),
        check_vma=False,
    )
```

profile of v0, /device:TPU:0, one launch (start us, length us, event | category | flops | bytes accessed | tf_op | source)
XLA Modules:
  0.0 1089.4 jit_solution(527268343555547212)
XLA Ops:
  12.4 68.5 %all-reduce.10 = (bf16[1024]{0:T(1024)(128)(2,1)S(1)}, bf16[1024]{0:T(1024)(128)(2,1)S(1)}) all-reduce(bf16[1024]{0:T(1024)(128)(2,1)S(1)} %dynamic-update-slice.1, bf16[1024]{0:T(1024)(128)(2,1)S(1)} %dynamic-update-slice), channel_id=1, replica_groups=mesh['dp'=4,'seq'=8,'tensor'=4] {'dp','seq'}, use_global_device_ids=true, to_apply=%add.5 | all-reduce | flops 2048 | bytes 8192
  80.9 22.4 %all_gather.46 = bf16[1024,128]{1,0:T(8,128)(2,1)S(1)} all-gather(bf16[32,128]{1,0:T(8,128)(2,1)} %param.23), channel_id=1, replica_groups=mesh['dp'=4,'seq'=8,'tensor'=4] {'dp','seq'}, dimensions={0}, use_global_device_ids=true | all-gather | bytes 270336 | tf_op jit(solution)/shard_map/all_gather | solution.py:73
  103.3 24.3 %all_gather.47 = bf16[1024,128]{1,0:T(8,128)(2,1)S(1)} all-gather(bf16[32,128]{1,0:T(8,128)(2,1)} %param.24), channel_id=1, replica_groups=mesh['dp'=4,'seq'=8,'tensor'=4] {'dp','seq'}, dimensions={0}, use_global_device_ids=true | all-gather | bytes 270336 | tf_op jit(solution)/shard_map/all_gather | solution.py:74
  127.6 13.7 %all_gather.44 = bf16[256,1,1024]{2,0,1:T(8,128)(2,1)S(1)} all-gather(bf16[256,1,256]{2,0,1:T(8,128)(2,1)} %param.17), channel_id=1, replica_groups=mesh['dp'=4,'seq'=8,'tensor'=4] {'tensor'}, dimensions={2}, use_global_device_ids=true | all-gather | bytes 655360 | tf_op jit(solution)/shard_map/all_gather | solution.py:60
  145.0 22.4 %all_gather.49 = bf16[1024,256]{1,0:T(8,128)(2,1)S(1)} all-gather(bf16[32,256]{1,0:T(8,128)(2,1)S(1)} %copy-done.34), channel_id=1, replica_groups=mesh['dp'=4,'seq'=8,'tensor'=4] {'dp','seq'}, dimensions={0}, use_global_device_ids=true | all-gather | bytes 540672 | tf_op jit(solution)/shard_map/all_gather | solution.py:72
  168.9 24.4 %all_gather.50 = bf16[1024,256]{1,0:T(8,128)(2,1)S(1)} all-gather(bf16[32,256]{1,0:T(8,128)(2,1)S(1)} %copy-done.35), channel_id=1, replica_groups=mesh['dp'=4,'seq'=8,'tensor'=4] {'dp','seq'}, dimensions={0}, use_global_device_ids=true | all-gather | bytes 540672 | tf_op jit(solution)/shard_map/all_gather | solution.py:75
  193.3 8.4 conditional.2
  205.5 14.8 %all_gather.55 = bf16[256,1,1024]{2,0,1:T(8,128)(2,1)S(1)} all-gather(bf16[256,1,256]{2,0,1:T(8,128)(2,1)S(1)} %copy-done.27), channel_id=1, replica_groups=mesh['dp'=4,'seq'=8,'tensor'=4] {'tensor'}, dimensions={2}, use_global_device_ids=true | all-gather | bytes 655360 | tf_op jit(solution)/shard_map/all_gather | solution.py:192
  220.2 25.8 %all-reduce.15.cloned.1.call-done = bf16[256,1024]{1,0:T(8,128)(2,1)} async-done(((bf16[256,1024]{1,0:T(8,128)(2,1)}), bf16[256,1024]{1,0:T(8,128)(2,1)}) %all-reduce.15.cloned.1.call-update) | async-done | bytes 524304 | tf_op jit(solution)/shard_map/psum | solution.py:164
  249.3 3.6 fusion.106
  252.9 42.1 %all-gather.7.cloned.1.call-done = bf16[1024,1152]{1,0:T(8,128)(2,1)} async-done(((bf16[32,1152]{1,0:T(8,128)(2,1)}), bf16[1024,1152]{1,0:T(8,128)(2,1)}) %all-gather.7.cloned.1.call-update) | async-done | bytes 2359312 | tf_op jit(solution)/shard_map/all_gather | solution.py:76
  295.0 3.6 fusion.105
  298.6 42.1 %all-gather.11.cloned.1.call-done = bf16[1024,1152]{1,0:T(8,128)(2,1)} async-done(((bf16[32,1152]{1,0:T(8,128)(2,1)}), bf16[1024,1152]{1,0:T(8,128)(2,1)}) %all-gather.11.cloned.1.call-update) | async-done | bytes 2359312 | tf_op jit(solution)/shard_map/all_gather | solution.py:78
  340.7 4.4 multiply_convert_fusion
  349.2 42.2 %all-reduce.17.cloned.1.call-done = bf16[256,1024]{1,0:T(8,128)(2,1)} async-done(((bf16[256,1024]{1,0:T(8,128)(2,1)}), bf16[256,1024]{1,0:T(8,128)(2,1)}) %all-reduce.17.cloned.1.call-update) | async-done | bytes 524304 | tf_op jit(solution)/shard_map/psum | solution.py:199
  394.2 2.5 fusion.69
  397.1 15.4 %conditional.3 = (bf16[2048,1,256]{0,2,1:T(8,128)(2,1)}, f32[256,1,4,32]{0,3,2,1:T(8,128)S(1)}, f32[256,1,4,32]{0,3,2,1:T(8,128)S(1)}, f32[256,1,4,32]{0,3,2,1:T(8,128)S(1)}) conditional(s32[]{:T(128)} %convert_element_type.243, () %tuple.37, (s32[256]{0:T(256)}, bf16[2048,1,256]{0,2,1:T(8,128)(2,1)}, bf16[256,1,2,2,64]{0,4,3,2,1:T(8,128)(2,1)}, ...), branch_computations={%region_12.13_spmd, %region_13.15_spmd} | conditional | flops 1366589440 | bytes 49067068 | solution.py:255
  405.3 2.9 fusion.18
  413.2 3.5 fusion.50
  421.4 24.7 %reduce-scatter.14.cloned.1.call-done = bf16[256,1,256]{0,2,1:T(8,128)(2,1)} async-done(((bf16[2048,1,256]{0,2,1:T(8,128)(2,1)}), bf16[256,1,256]{0,2,1:T(8,128)(2,1)}) %reduce-scatter.14.cloned.1.call-update) | async-done | bytes 131088 | tf_op jit(solution)/shard_map/reduce_scatter | solution.py:258
  459.1 3.3 fusion.44
  462.4 4.3 copy.50
  475.1 73.5 %reduce-scatter.22.cloned.1.call-done = bf16[32,256]{1,0:T(8,128)(2,1)} async-done(((bf16[1024,256]{1,0:T(8,128)(2,1)}), bf16[32,256]{1,0:T(8,128)(2,1)}) %reduce-scatter.22.cloned.1.call-update) | async-done | bytes 16400 | tf_op jit(solution)/shard_map/reduce_scatter | solution.py:303
  549.9 78.5 %reduce-scatter.16.cloned.1.call-done = bf16[32,256]{1,0:T(8,128)(2,1)} async-done(((bf16[1024,256]{1,0:T(8,128)(2,1)}), bf16[32,256]{1,0:T(8,128)(2,1)}) %reduce-scatter.16.cloned.1.call-update) | async-done | bytes 16400 | tf_op jit(solution)/shard_map/reduce_scatter | solution.py:294
  629.8 64.6 %all-reduce.8 = (f32[64]{0:T(128)}, f32[64]{0:T(128)}) all-reduce(f32[64]{0:T(128)S(1)} %copy-done.52, f32[64]{0:T(128)S(1)} %copy-done.51), channel_id=1, replica_groups=mesh['dp'=4,'seq'=8,'tensor'=4] {'dp','seq','tensor'}, use_global_device_ids=true, to_apply=%region_25.26 | all-reduce | flops 128 | bytes 1024 | tf_op jit(solution)/shard_map/psum | solution.py:316
  694.4 13.8 %reduce-scatter.18.cloned.1.call-done = bf16[32,128]{1,0:T(8,128)(2,1)} async-done(((bf16[1024,128]{1,0:T(8,128)(2,1)}), bf16[32,128]{1,0:T(8,128)(2,1)}) %reduce-scatter.18.cloned.1.call-update) | async-done | bytes 8208 | tf_op jit(solution)/shard_map/reduce_scatter | solution.py:297
  709.4 78.4 %reduce-scatter.20.cloned.1.call-done = bf16[32,128]{1,0:T(8,128)(2,1)} async-done(((bf16[1024,128]{1,0:T(8,128)(2,1)}), bf16[32,128]{1,0:T(8,128)(2,1)}) %reduce-scatter.20.cloned.1.call-update) | async-done | bytes 8208 | tf_op jit(solution)/shard_map/reduce_scatter | solution.py:300
  789.2 43.1 %all-reduce.19.cloned.1.call-done = bf16[256,1024]{1,0:T(8,128)(2,1)} async-done(((bf16[256,1024]{1,0:T(8,128)(2,1)}), bf16[256,1024]{1,0:T(8,128)(2,1)}) %all-reduce.19.cloned.1.call-update) | async-done | bytes 524304 | tf_op jit(solution)/shard_map/psum | solution.py:270
  834.7 65.3 %all-reduce.9 = (bf16[1024]{0:T(1024)(128)(2,1)S(1)}, bf16[1024]{0:T(1024)(128)(2,1)S(1)}) all-reduce(bf16[1024]{0:T(1024)(128)(2,1)S(1)} %get-tuple-element.145, bf16[1024]{0:T(1024)(128)(2,1)S(1)} %copy-done.45), channel_id=4, replica_groups=mesh['dp'=4,'seq'=8,'tensor'=4] {'dp','seq'}, use_global_device_ids=true, to_apply=%region_21.22.clone | all-reduce | flops 2048 | bytes 8192
  902.4 13.4 %reduce-scatter.28.cloned.1.call-done = bf16[32,1152]{1,0:T(8,128)(2,1)} async-done(((bf16[1024,1152]{1,0:T(8,128)(2,1)}), bf16[32,1152]{1,0:T(8,128)(2,1)}) %reduce-scatter.28.cloned.1.call-update) | async-done | bytes 73744
  917.7 80.6 %reduce-scatter.26.cloned.1.call-done = bf16[32,1152]{1,0:T(8,128)(2,1)} async-done(((bf16[1024,1152]{1,0:T(8,128)(2,1)}), bf16[32,1152]{1,0:T(8,128)(2,1)}) %reduce-scatter.26.cloned.1.call-update) | async-done | bytes 73744 | tf_op jit(solution)/shard_map/reduce_scatter | solution.py:309
  999.8 80.7 %reduce-scatter.24.cloned.1.call-done = bf16[32,1152]{1,0:T(8,128)(2,1)} async-done(((bf16[1024,1152]{1,0:T(8,128)(2,1)}), bf16[32,1152]{1,0:T(8,128)(2,1)}) %reduce-scatter.24.cloned.1.call-update) | async-done | bytes 73744 | tf_op jit(solution)/shard_map/reduce_scatter | solution.py:306
  (232 shorter events, 84.3 us)
Async XLA Ops:
  8.0 185.3 %all-gather.5.cloned.1.call-start = ((), (), s32[]{:S(2)}) async-start(), calls=%async_computation.9 | async-start | bytes 1179648 | tf_op jit(solution)/shard_map/all_gather | solution.py:141
  8.8 134.5 %copy-start.46 = (f32[64]{0:T(128)}, f32[64]{0:T(128)S(1)}, u32[]{:S(2)}) copy-start(f32[64]{0:T(128)S(1)} %convert_element_type.246) | copy-start | bytes 772
  80.9 86.5 %copy-start.32 = (f32[1024]{0:T(1024)}, f32[1024]{0:T(1024)S(1)}, u32[]{:S(2)}) copy-start(f32[1024]{0:T(1024)S(1)} %convert_element_type.244) | copy-start | bytes 12292
  103.3 40.9 %copy-start.15 = (bf16[1024,128]{1,0:T(8,128)(2,1)}, bf16[1024,128]{1,0:T(8,128)(2,1)S(1)}, u32[]{:S(2)}) copy-start(bf16[1024,128]{1,0:T(8,128)(2,1)S(1)} %all_gather.46) | copy-start | bytes 786436
  143.2 50.1 %copy-start.16 = (f32[256,32]{0,1:T(8,128)}, f32[256,32]{0,1:T(8,128)S(1)}, u32[]{:S(2)}) copy-start(f32[256,32]{0,1:T(8,128)S(1)} %get-tuple-element.184) | copy-start | bytes 98308
  143.2 50.1 %copy-start.18 = (f32[256,32]{0,1:T(8,128)}, f32[256,32]{0,1:T(8,128)S(1)}, u32[]{:S(2)}) copy-start(f32[256,32]{0,1:T(8,128)S(1)} %get-tuple-element.185) | copy-start | bytes 98308
  144.3 101.8 %all-reduce.15.cloned.1.call-start = ((), (), s32[]{:S(2)}) async-start(), calls=%async_computation.10 | async-start | bytes 1048576 | tf_op jit(solution)/shard_map/psum | solution.py:164
  144.4 48.9 %copy-start.48 = (f32[64]{0:T(128)}, f32[64]{0:T(128)S(1)}, u32[]{:S(2)}) copy-start(f32[64]{0:T(128)S(1)} %convert_element_type.250) | copy-start | bytes 772
  202.5 46.2 %copy-start.11 = (bf16[256,1,2,2,64]{0,4,3,2,1:T(8,128)(2,1)}, bf16[256,1,2,2,64]{0,4,3,2,1:T(8,128)(2,1)S(1)}, u32[]{:S(2)}) copy-start(bf16[256,1,2,2,64]{0,4,3,2,1:T(8,128)(2,1)S(1)} %get-tuple-element.159) | copy-start | bytes 393220
  203.6 45.6 %all-gather.9.cloned.1.call-start = ((), (), s32[]{:S(2)}) async-start(), calls=%async_computation.12 | async-start | bytes 2433024 | tf_op jit(solution)/shard_map/all_gather | solution.py:77
  204.2 90.8 %all-gather.7.cloned.1.call-start = ((), (), s32[]{:S(2)}) async-start(), calls=%async_computation.11 | async-start | bytes 2433024 | tf_op jit(solution)/shard_map/all_gather | solution.py:76
  204.8 135.9 %all-gather.11.cloned.1.call-start = ((), (), s32[]{:S(2)}) async-start(), calls=%async_computation.13 | async-start | bytes 2433024 | tf_op jit(solution)/shard_map/all_gather | solution.py:78
  205.4 186.0 %all-reduce.17.cloned.1.call-start = ((), (), s32[]{:S(2)}) async-start(), calls=%async_computation.15 | async-start | bytes 1048576 | tf_op jit(solution)/shard_map/psum | solution.py:199
  347.2 44.1 %copy-start.2 = (bf16[256,1024]{1,0:T(8,128)(2,1)S(1)}, bf16[256,1024]{1,0:T(8,128)(2,1)}, u32[]{:S(2)}) copy-start(bf16[256,1024]{1,0:T(8,128)(2,1)} %all-reduce.15.cloned.1.call-done) | copy-start | bytes 1572868
  348.9 97.1 %reduce-scatter.14.cloned.1.call-start = ((), (), s32[]{:S(2)}) async-start(), calls=%async_computation.16 | async-start | bytes 1179648 | tf_op jit(solution)/shard_map/reduce_scatter | solution.py:258
  413.2 60.2 %reduce-scatter.12.cloned.1.call-start = ((), (), s32[]{:S(2)}) async-start(), calls=%async_computation.14 | async-start | bytes 655360 | tf_op jit(solution)/shard_map/reduce_scatter | solution.py:172
  416.9 131.7 %reduce-scatter.22.cloned.1.call-start = ((), (), s32[]{:S(2)}) async-start(), calls=%async_computation.21 | async-start | bytes 540672 | tf_op jit(solution)/shard_map/reduce_scatter | solution.py:303
  418.1 28.9 %copy-start.29 = (f32[256,2]{0,1:T(2,128)S(1)}, f32[256,2]{0,1:T(2,128)}, u32[]{:S(2)}) copy-start(f32[256,2]{0,1:T(2,128)} %copy-done.28) | copy-start | bytes 6148
  418.1 28.9 %copy-start.47 = (f32[64]{0:T(128)S(1)}, f32[64]{0:T(128)}, u32[]{:S(2)}) copy-start(f32[64]{0:T(128)} %copy-done.46) | copy-start | bytes 772
  418.1 29.5 %copy-start.31 = (f32[256,2]{0,1:T(2,128)S(1)}, f32[256,2]{0,1:T(2,128)}, u32[]{:S(2)}) copy-start(f32[256,2]{0,1:T(2,128)} %copy-done.30) | copy-start | bytes 6148
  418.1 210.3 %reduce-scatter.16.cloned.1.call-start = ((), (), s32[]{:S(2)}) async-start(), calls=%async_computation.18 | async-start | bytes 540672 | tf_op jit(solution)/shard_map/reduce_scatter | solution.py:294
  420.0 30.9 %copy-start.41 = (f32[256]{0:T(256)S(1)}, f32[256]{0:T(256)}, u32[]{:S(2)}) copy-start(f32[256]{0:T(256)} %copy-done.39) | copy-start | bytes 3076
  421.4 286.8 %reduce-scatter.18.cloned.1.call-start = ((), (), s32[]{:S(2)}) async-start(), calls=%async_computation.19 | async-start | bytes 270336 | tf_op jit(solution)/shard_map/reduce_scatter | solution.py:297
  450.9 337.0 %reduce-scatter.20.cloned.1.call-start = ((), (), s32[]{:S(2)}) async-start(), calls=%async_computation.20 | async-start | bytes 270336 | tf_op jit(solution)/shard_map/reduce_scatter | solution.py:300
  455.3 376.9 %all-reduce.19.cloned.1.call-start = ((), (), s32[]{:S(2)}) async-start(), calls=%async_computation.17 | async-start | bytes 1048576 | tf_op jit(solution)/shard_map/psum | solution.py:270
  459.0 456.8 %reduce-scatter.28.cloned.1.call-start = ((), (), s32[]{:S(2)}) async-start(), calls=%async_computation.24 | async-start | bytes 2433024
  466.7 531.6 %reduce-scatter.26.cloned.1.call-start = ((), (), s32[]{:S(2)}) async-start(), calls=%async_computation.23 | async-start | bytes 2433024 | tf_op jit(solution)/shard_map/reduce_scatter | solution.py:309
  470.1 610.4 %reduce-scatter.24.cloned.1.call-start = ((), (), s32[]{:S(2)}) async-start(), calls=%async_computation.22 | async-start | bytes 2433024 | tf_op jit(solution)/shard_map/reduce_scatter | solution.py:306
  472.5 157.3 %copy-start.51 = (f32[64]{0:T(128)S(1)}, f32[64]{0:T(128)}, u32[]{:S(2)}) copy-start(f32[64]{0:T(128)} %get-tuple-element.149) | copy-start | bytes 772
  472.5 157.3 %copy-start.52 = (f32[64]{0:T(128)S(1)}, f32[64]{0:T(128)}, u32[]{:S(2)}) copy-start(f32[64]{0:T(128)} %get-tuple-element.147) | copy-start | bytes 772
  472.5 362.2 %copy-start.45 = (bf16[1024]{0:T(1024)(128)(2,1)S(1)}, bf16[1024]{0:T(1024)(128)(2,1)}, u32[]{:S(2)}) copy-start(bf16[1024]{0:T(1024)(128)(2,1)} %get-tuple-element.143) | copy-start | bytes 6148
  472.5 428.1 %copy-start.43 = (f32[256]{0:T(256)S(1)}, f32[256]{0:T(256)}, u32[]{:S(2)}) copy-start(f32[256]{0:T(256)} %copy-done.42) | copy-start | bytes 3076
  (38 other events, 223.7 us)
Sparse Core Ops, SparseCore 0:
  144.4 22.6 all-gather.4
  203.8 42.2 all-reduce.14
  349.1 42.2 all-reduce.16
  413.3 32.7 reduce-scatter.13
  448.3 20.0 reduce-scatter.11
  471.7 76.8 reduce-scatter.21
  552.0 76.3 reduce-scatter.15
  631.9 76.2 reduce-scatter.17
  711.6 76.2 reduce-scatter.19
  790.0 42.1 all-reduce.18
  835.8 79.9 reduce-scatter.27
  919.6 78.6 reduce-scatter.25
  1001.9 78.5 reduce-scatter.23
Sparse Core Ops, SparseCore 1:
  206.4 42.8 all-gather.8
  251.4 43.6 all-gather.6
  297.1 43.6 all-gather.10
where the time goes:
time: 1090 us
  waiting for transfers between devices  641 us (59%)
  blocking collectives  320 us (29%)
  matrix products  55 us (5%)
  other arithmetic  36.8 us (3%)
  between operations  17.6 us (2%)
  local copies, waits for them, and re-layouts  17.2 us (2%)
    unnamed x2, blocking collectives  134 us
    reduce_scatter x1, waiting for transfers between devices, body(): lax.psum_scatter(gate_sum.astype(jnp.bfloat16), ('dp', 'seq'), scatter_di...  80.7 us
    reduce_scatter x1, waiting for transfers between devices, body(): lax.psum_scatter(up_sum.astype(jnp.bfloat16), ('dp', 'seq'), scatter_dime...  80.6 us
    reduce_scatter x1, waiting for transfers between devices, body(): lax.psum_scatter(query_sum.astype(jnp.bfloat16), ('dp', 'seq'), scatter_d...  78.5 us
    reduce_scatter x1, waiting for transfers between devices, body(): lax.psum_scatter(value_sum.astype(jnp.bfloat16), ('dp', 'seq'), scatter_d...  78.4 us
    reduce_scatter x1, waiting for transfers between devices, body(): lax.psum_scatter(out_sum.astype(jnp.bfloat16), ('dp', 'seq'), scatter_dim...  73.5 us
    psum x1, blocking collectives, body(): lax.psum((query_gain_part, key_gain_part), ('dp', 'seq', 'tensor'))  64.6 us
    psum x1, waiting for transfers between devices, body(): lax.psum((contract_cols(query_gb, query_back) + contract_cols(key_gb, key...  43.1 us
  transfers between devices with their start and end apart: 16, of which 14 were waited for; matrix products, arithmetic and copies ran while one was open for 5% of the time, Pallas kernels for 0%

commit v1 on v0

--- a/solution.py
+++ b/solution.py
@@ -267,13 +267,16 @@
     query_gb = query_raw_grad.astype(jnp.bfloat16)
     key_gb = key_raw_grad.astype(jnp.bfloat16)
     value_gb = kv_mine[..., kv_width:].reshape(row_count, kv_width).astype(jnp.bfloat16)
-    normed_one_grad = lax.psum(
-        (
-            contract_cols(query_gb, query_back)
-            + contract_cols(key_gb, key_back)
-            + contract_cols(value_gb, value_back)
-        ).astype(jnp.bfloat16),
-        "tensor",
+    normed_one_grad = jnp.sum(
+        lax.all_gather(
+            (
+                contract_cols(query_gb, query_back)
+                + contract_cols(key_gb, key_back)
+                + contract_cols(value_gb, value_back)
+            ).astype(jnp.bfloat16),
+            "tensor",
+        ),
+        axis=0,
     ).astype(jnp.float32)
     query_sum = contract_rows(normed_one, query_gb)
     key_sum = contract_rows(normed_one, key_gb)

time: 1090 us -> 1140 us (1.046)
  waiting for transfers between devices: 641 us -> 702 us
    unnamed x17, waiting for transfers between devices: 15.2 us -> 82.6 us
    psum x1 -> x0, waiting for transfers between devices: 43.1 us -> none  [body(): lax.psum((contract_cols(query_gb, query_back) + contract_cols(key_gb, key...]
    all_gather x1, waiting for transfers between devices: 42.1 us -> 0.56 us  [body(): lax.all_gather(gate_weight, ('dp', 'seq'), axis=0, tiled=True)]
    all_gather x1, waiting for transfers between devices: 0.59 us -> 42.1 us  [body(): lax.all_gather(up_weight, ('dp', 'seq'), axis=0, tiled=True)]
    all_gather x0 -> x1, waiting for transfers between devices: none -> 30.4 us  [body(): lax.all_gather((contract_cols(query_gb, query_back) + contract_cols(key_g...]
  transfers between devices with their start and end apart: 16 -> 16, of which waited for: 14 -> 15; matrix products, arithmetic and copies ran while one was open for 5% -> 4% of each run, Pallas kernels for 0% -> 0%
where the time goes in v1:
time: 1140 us
  waiting for transfers between devices  702 us (62%)
  blocking collectives  318 us (28%)
  matrix products  49.2 us (4%)
  other arithmetic  34.9 us (3%)
  local copies, waits for them, and re-layouts  18.6 us (2%)
  between operations  17.6 us (2%)
    unnamed x2, blocking collectives  131 us
    unnamed x17, waiting for transfers between devices  82.6 us
    reduce_scatter x1, waiting for transfers between devices, body(): lax.psum_scatter(gate_sum.astype(jnp.bfloat16), ('dp', 'seq'), scatter_di...  80.7 us
    reduce_scatter x1, waiting for transfers between devices, body(): lax.psum_scatter(up_sum.astype(jnp.bfloat16), ('dp', 'seq'), scatter_dime...  80.5 us
    reduce_scatter x1, waiting for transfers between devices, body(): lax.psum_scatter(query_sum.astype(jnp.bfloat16), ('dp', 'seq'), scatter_d...  78.5 us
    reduce_scatter x1, waiting for transfers between devices, body(): lax.psum_scatter(out_sum.astype(jnp.bfloat16), ('dp', 'seq'), scatter_dim...  78.5 us
    reduce_scatter x1, waiting for transfers between devices, body(): lax.psum_scatter(value_sum.astype(jnp.bfloat16), ('dp', 'seq'), scatter_d...  78.4 us
    psum x1, blocking collectives, body(): lax.psum((query_gain_part, key_gain_part), ('dp', 'seq', 'tensor'))  64.6 us
  transfers between devices with their start and end apart: 16, of which 15 were waited for; matrix products, arithmetic and copies ran while one was open for 4% of the time, Pallas kernels for 0%

profile of v1, /device:TPU:0, one launch (start us, length us, event | category | flops | bytes accessed | tf_op | source)
XLA Modules:
  0.0 1142.0 jit_solution(10248904072086999529)
XLA Ops:
  8.1 26.2 %all_gather.53 = bf16[1024,128]{1,0:T(8,128)(2,1)S(1)} all-gather(bf16[32,128]{1,0:T(8,128)(2,1)} %param.24), channel_id=1, replica_groups=mesh['dp'=4,'seq'=8,'tensor'=4] {'dp','seq'}, dimensions={0}, use_global_device_ids=true | all-gather | bytes 270336 | tf_op jit(solution)/shard_map/all_gather | solution.py:74
  34.3 13.7 %all_gather.50 = bf16[256,1,1024]{2,0,1:T(8,128)(2,1)S(1)} all-gather(bf16[256,1,256]{2,0,1:T(8,128)(2,1)} %param.17), channel_id=1, replica_groups=mesh['dp'=4,'seq'=8,'tensor'=4] {'tensor'}, dimensions={2}, use_global_device_ids=true | all-gather | bytes 655360 | tf_op jit(solution)/shard_map/all_gather | solution.py:60
  51.7 63.3 %all-reduce.10 = (bf16[1024]{0:T(1024)(128)(2,1)S(1)}, bf16[1024]{0:T(1024)(128)(2,1)S(1)}) all-reduce(bf16[1024]{0:T(1024)(128)(2,1)S(1)} %dynamic-update-slice.1, bf16[1024]{0:T(1024)(128)(2,1)S(1)} %dynamic-update-slice), channel_id=1, replica_groups=mesh['dp'=4,'seq'=8,'tensor'=4] {'dp','seq'}, use_global_device_ids=true, to_apply=%add.5 | all-reduce | flops 2048 | bytes 8192
  116.5 22.4 %all_gather.52 = bf16[1024,128]{1,0:T(8,128)(2,1)S(1)} all-gather(bf16[32,128]{1,0:T(8,128)(2,1)} %param.23), channel_id=1, replica_groups=mesh['dp'=4,'seq'=8,'tensor'=4] {'dp','seq'}, dimensions={0}, use_global_device_ids=true | all-gather | bytes 270336 | tf_op jit(solution)/shard_map/all_gather | solution.py:73
  141.7 24.2 %all_gather.55 = bf16[1024,256]{1,0:T(8,128)(2,1)S(1)} all-gather(bf16[32,256]{1,0:T(8,128)(2,1)S(1)} %copy-done.38), channel_id=1, replica_groups=mesh['dp'=4,'seq'=8,'tensor'=4] {'dp','seq'}, dimensions={0}, use_global_device_ids=true | all-gather | bytes 540672 | tf_op jit(solution)/shard_map/all_gather | solution.py:72
  167.4 22.6 %all_gather.56 = bf16[1024,256]{1,0:T(8,128)(2,1)S(1)} all-gather(bf16[32,256]{1,0:T(8,128)(2,1)S(1)} %copy-done.39), channel_id=1, replica_groups=mesh['dp'=4,'seq'=8,'tensor'=4] {'dp','seq'}, dimensions={0}, use_global_device_ids=true | all-gather | bytes 540672 | tf_op jit(solution)/shard_map/all_gather | solution.py:75
  190.0 8.4 conditional.2
  192.4 2.4 fusion
  202.2 14.0 %all_gather.61 = bf16[256,1,1024]{2,0,1:T(8,128)(2,1)S(1)} all-gather(bf16[256,1,256]{2,0,1:T(8,128)(2,1)S(1)} %copy-done.31), channel_id=1, replica_groups=mesh['dp'=4,'seq'=8,'tensor'=4] {'tensor'}, dimensions={2}, use_global_device_ids=true | all-gather | bytes 655360 | tf_op jit(solution)/shard_map/all_gather | solution.py:192
  216.2 26.8 %all-reduce.14.cloned.1.call-done = bf16[256,1024]{1,0:T(8,128)(2,1)} async-done(((bf16[256,1024]{1,0:T(8,128)(2,1)}), bf16[256,1024]{1,0:T(8,128)(2,1)}) %all-reduce.14.cloned.1.call-update) | async-done | bytes 524304 | tf_op jit(solution)/shard_map/psum | solution.py:164
  246.1 3.6 fusion.105
  249.7 42.1 %all-gather.11.cloned.1.call-done = bf16[1024,1152]{1,0:T(8,128)(2,1)} async-done(((bf16[32,1152]{1,0:T(8,128)(2,1)}), bf16[1024,1152]{1,0:T(8,128)(2,1)}) %all-gather.11.cloned.1.call-update) | async-done | bytes 2359312 | tf_op jit(solution)/shard_map/all_gather | solution.py:77
  291.9 3.6 fusion.106
  295.4 42.2 %all-gather.13.cloned.1.call-done = bf16[1024,1152]{1,0:T(8,128)(2,1)} async-done(((bf16[32,1152]{1,0:T(8,128)(2,1)}), bf16[1024,1152]{1,0:T(8,128)(2,1)}) %all-gather.13.cloned.1.call-update) | async-done | bytes 2359312 | tf_op jit(solution)/shard_map/all_gather | solution.py:78
  337.6 4.4 multiply_convert_fusion
  346.1 42.2 %all-reduce.16.cloned.1.call-done = bf16[256,1024]{1,0:T(8,128)(2,1)} async-done(((bf16[256,1024]{1,0:T(8,128)(2,1)}), bf16[256,1024]{1,0:T(8,128)(2,1)}) %all-reduce.16.cloned.1.call-update) | async-done | bytes 524304 | tf_op jit(solution)/shard_map/psum | solution.py:199
  393.8 14.6 %conditional.3 = (bf16[2048,1,256]{0,2,1:T(8,128)(2,1)}, f32[256,1,4,32]{0,3,2,1:T(8,128)S(1)}, f32[256,1,4,32]{0,3,2,1:T(8,128)S(1)}, f32[256,1,4,32]{0,3,2,1:T(8,128)S(1)}) conditional(s32[]{:T(128)} %convert_element_type.245, () %tuple.37, (s32[256]{0:T(256)}, bf16[2048,1,256]{0,2,1:T(8,128)(2,1)}, bf16[256,1,2,2,64]{0,4,3,2,1:T(8,128)(2,1)}, ...), branch_computations={%region_12.13_spmd, %region_13.15_spmd} | conditional | flops 1366589440 | bytes 52212880 | solution.py:255
  401.2 2.9 fusion.18
  409.0 3.6 fusion.50
  417.8 23.5 %reduce-scatter.14.cloned.1.call-done = bf16[256,1,256]{0,2,1:T(8,128)(2,1)} async-done(((bf16[2048,1,256]{0,2,1:T(8,128)(2,1)}), bf16[256,1,256]{0,2,1:T(8,128)(2,1)}) %reduce-scatter.14.cloned.1.call-update) | async-done | bytes 131088 | tf_op jit(solution)/shard_map/reduce_scatter | solution.py:258
  445.0 3.3 fusion.44
  448.3 4.3 copy.50
  465.3 78.5 %reduce-scatter.16.cloned.1.call-done = bf16[32,256]{1,0:T(8,128)(2,1)} async-done(((bf16[1024,256]{1,0:T(8,128)(2,1)}), bf16[32,256]{1,0:T(8,128)(2,1)}) %reduce-scatter.16.cloned.1.call-update) | async-done | bytes 16400 | tf_op jit(solution)/shard_map/reduce_scatter | solution.py:297
  545.2 78.5 %reduce-scatter.22.cloned.1.call-done = bf16[32,256]{1,0:T(8,128)(2,1)} async-done(((bf16[1024,256]{1,0:T(8,128)(2,1)}), bf16[32,256]{1,0:T(8,128)(2,1)}) %reduce-scatter.22.cloned.1.call-update) | async-done | bytes 16400 | tf_op jit(solution)/shard_map/reduce_scatter | solution.py:306
  625.0 64.6 %all-reduce.8 = (f32[64]{0:T(128)}, f32[64]{0:T(128)}) all-reduce(f32[64]{0:T(128)S(1)} %copy-done.54, f32[64]{0:T(128)S(1)} %get-tuple-element.149), channel_id=1, replica_groups=mesh['dp'=4,'seq'=8,'tensor'=4] {'dp','seq','tensor'}, use_global_device_ids=true, to_apply=%region_25.26 | all-reduce | flops 128 | bytes 1024 | tf_op jit(solution)/shard_map/psum | solution.py:319
  689.6 13.8 %reduce-scatter.18.cloned.1.call-done = bf16[32,128]{1,0:T(8,128)(2,1)} async-done(((bf16[1024,128]{1,0:T(8,128)(2,1)}), bf16[32,128]{1,0:T(8,128)(2,1)}) %reduce-scatter.18.cloned.1.call-update) | async-done | bytes 8208 | tf_op jit(solution)/shard_map/reduce_scatter | solution.py:300
  704.6 78.4 %reduce-scatter.20.cloned.1.call-done = bf16[32,128]{1,0:T(8,128)(2,1)} async-done(((bf16[1024,128]{1,0:T(8,128)(2,1)}), bf16[32,128]{1,0:T(8,128)(2,1)}) %reduce-scatter.20.cloned.1.call-update) | async-done | bytes 8208 | tf_op jit(solution)/shard_map/reduce_scatter | solution.py:303
  784.3 80.8 %reduce-scatter.28.cloned.1.call-done = bf16[32,1152]{1,0:T(8,128)(2,1)} async-done(((bf16[1024,1152]{1,0:T(8,128)(2,1)}), bf16[32,1152]{1,0:T(8,128)(2,1)}) %reduce-scatter.28.cloned.1.call-update) | async-done | bytes 73744
  867.0 80.7 %reduce-scatter.24.cloned.1.call-done = bf16[32,1152]{1,0:T(8,128)(2,1)} async-done(((bf16[1024,1152]{1,0:T(8,128)(2,1)}), bf16[32,1152]{1,0:T(8,128)(2,1)}) %reduce-scatter.24.cloned.1.call-update) | async-done | bytes 73744 | tf_op jit(solution)/shard_map/reduce_scatter | solution.py:309
  949.3 80.5 %reduce-scatter.26.cloned.1.call-done = bf16[32,1152]{1,0:T(8,128)(2,1)} async-done(((bf16[1024,1152]{1,0:T(8,128)(2,1)}), bf16[32,1152]{1,0:T(8,128)(2,1)}) %reduce-scatter.26.cloned.1.call-update) | async-done | bytes 73744 | tf_op jit(solution)/shard_map/reduce_scatter | solution.py:312
  1031.4 30.4 %all-gather.15.cloned.1.call-done = bf16[1024,1024]{1,0:T(8,128)(2,1)} async-done(((bf16[256,1024]{1,0:T(8,128)(2,1)}), bf16[1024,1024]{1,0:T(8,128)(2,1)}) %all-gather.15.cloned.1.call-update) | async-done | bytes 2097168 | tf_op jit(solution)/shard_map/all_gather | solution.py:271
  1065.1 67.2 %all-reduce.9 = (bf16[1024]{0:T(1024)(128)(2,1)S(1)}, bf16[1024]{0:T(1024)(128)(2,1)S(1)}) all-reduce(bf16[1024]{0:T(1024)(128)(2,1)S(1)} %get-tuple-element.145, bf16[1024]{0:T(1024)(128)(2,1)S(1)} %copy-done.49), channel_id=5, replica_groups=mesh['dp'=4,'seq'=8,'tensor'=4] {'dp','seq'}, use_global_device_ids=true, to_apply=%region_21.22.clone | all-reduce | flops 2048 | bytes 8192
  (237 shorter events, 79.8 us)
Async XLA Ops:
  8.0 182.0 %all-gather.7.cloned.1.call-start = ((), (), s32[]{:S(2)}) async-start(), calls=%async_computation.9 | async-start | bytes 1179648 | tf_op jit(solution)/shard_map/all_gather | solution.py:141
  34.3 106.7 %copy-start.16 = (bf16[1024,128]{1,0:T(8,128)(2,1)}, bf16[1024,128]{1,0:T(8,128)(2,1)S(1)}, u32[]{:S(2)}) copy-start(bf16[1024,128]{1,0:T(8,128)(2,1)S(1)} %all_gather.53) | copy-start | bytes 786436
  34.3 106.8 %copy-start.55 = (bf16[64]{0:T(256)(128)(2,1)S(1)}, bf16[64]{0:T(256)(128)(2,1)}, u32[]{:S(2)}) copy-start(bf16[64]{0:T(256)(128)(2,1)} %param.20) | copy-start | bytes 388
  34.3 107.4 %copy-start.38 = (bf16[32,256]{1,0:T(8,128)(2,1)S(1)}, bf16[32,256]{1,0:T(8,128)(2,1)}, u32[]{:S(2)}) copy-start(bf16[32,256]{1,0:T(8,128)(2,1)} %param.22) | copy-start | bytes 49156
  115.1 50.9 %copy-start.36 = (f32[1024]{0:T(1024)}, f32[1024]{0:T(1024)S(1)}, u32[]{:S(2)}) copy-start(f32[1024]{0:T(1024)S(1)} %convert_element_type.246) | copy-start | bytes 12292
  115.8 50.6 %copy-start.43 = (f32[256]{0:T(256)}, f32[256]{0:T(256)S(1)}, u32[]{:S(2)}) copy-start(f32[256]{0:T(256)S(1)} %fusion.89) | copy-start | bytes 3076
  139.7 27.7 %copy-start.39 = (bf16[32,256]{1,0:T(8,128)(2,1)S(1)}, bf16[32,256]{1,0:T(8,128)(2,1)}, u32[]{:S(2)}) copy-start(bf16[32,256]{1,0:T(8,128)(2,1)} %param.25) | copy-start | bytes 49156
  140.0 50.0 %copy-start.20 = (f32[256,32]{0,1:T(8,128)}, f32[256,32]{0,1:T(8,128)S(1)}, u32[]{:S(2)}) copy-start(f32[256,32]{0,1:T(8,128)S(1)} %get-tuple-element.184) | copy-start | bytes 98308
  140.0 50.0 %copy-start.22 = (f32[256,32]{0,1:T(8,128)}, f32[256,32]{0,1:T(8,128)S(1)}, u32[]{:S(2)}) copy-start(f32[256,32]{0,1:T(8,128)S(1)} %get-tuple-element.185) | copy-start | bytes 98308
  141.0 101.9 %all-reduce.14.cloned.1.call-start = ((), (), s32[]{:S(2)}) async-start(), calls=%async_computation.10 | async-start | bytes 1048576 | tf_op jit(solution)/shard_map/psum | solution.py:164
  141.1 48.9 %copy-start.52 = (f32[64]{0:T(128)}, f32[64]{0:T(128)S(1)}, u32[]{:S(2)}) copy-start(f32[64]{0:T(128)S(1)} %convert_element_type.252) | copy-start | bytes 772
  199.2 46.4 %copy-start.13 = (bf16[256,1,2,2,64]{0,4,3,2,1:T(8,128)(2,1)}, bf16[256,1,2,2,64]{0,4,3,2,1:T(8,128)(2,1)S(1)}, u32[]{:S(2)}) copy-start(bf16[256,1,2,2,64]{0,4,3,2,1:T(8,128)(2,1)S(1)} %get-tuple-element.159) | copy-start | bytes 393220
  200.4 45.8 %all-gather.9.cloned.1.call-start = ((), (), s32[]{:S(2)}) async-start(), calls=%async_computation.11 | async-start | bytes 2433024 | tf_op jit(solution)/shard_map/all_gather | solution.py:76
  200.9 90.9 %all-gather.11.cloned.1.call-start = ((), (), s32[]{:S(2)}) async-start(), calls=%async_computation.12 | async-start | bytes 2433024 | tf_op jit(solution)/shard_map/all_gather | solution.py:77
  201.5 136.1 %all-gather.13.cloned.1.call-start = ((), (), s32[]{:S(2)}) async-start(), calls=%async_computation.13 | async-start | bytes 2433024 | tf_op jit(solution)/shard_map/all_gather | solution.py:78
  202.1 186.1 %all-reduce.16.cloned.1.call-start = ((), (), s32[]{:S(2)}) async-start(), calls=%async_computation.15 | async-start | bytes 1048576 | tf_op jit(solution)/shard_map/psum | solution.py:199
  344.1 44.1 %copy-start.2 = (bf16[256,1024]{1,0:T(8,128)(2,1)S(1)}, bf16[256,1024]{1,0:T(8,128)(2,1)}, u32[]{:S(2)}) copy-start(bf16[256,1024]{1,0:T(8,128)(2,1)} %all-reduce.14.cloned.1.call-done) | copy-start | bytes 1572868
  345.8 95.5 %reduce-scatter.14.cloned.1.call-start = ((), (), s32[]{:S(2)}) async-start(), calls=%async_computation.16 | async-start | bytes 1179648 | tf_op jit(solution)/shard_map/reduce_scatter | solution.py:258
  408.4 55.2 %reduce-scatter.12.cloned.1.call-start = ((), (), s32[]{:S(2)}) async-start(), calls=%async_computation.14 | async-start | bytes 655360 | tf_op jit(solution)/shard_map/reduce_scatter | solution.py:172
  412.6 131.3 %reduce-scatter.16.cloned.1.call-start = ((), (), s32[]{:S(2)}) async-start(), calls=%async_computation.17 | async-start | bytes 540672 | tf_op jit(solution)/shard_map/reduce_scatter | solution.py:297
  414.5 27.7 %copy-start.33 = (f32[256,2]{0,1:T(2,128)S(1)}, f32[256,2]{0,1:T(2,128)}, u32[]{:S(2)}) copy-start(f32[256,2]{0,1:T(2,128)} %copy-done.32) | copy-start | bytes 6148
  414.6 27.7 %copy-start.51 = (f32[64]{0:T(128)S(1)}, f32[64]{0:T(128)}, u32[]{:S(2)}) copy-start(f32[64]{0:T(128)} %copy-done.50) | copy-start | bytes 772
  415.2 27.2 %copy-start.35 = (f32[256,2]{0,1:T(2,128)S(1)}, f32[256,2]{0,1:T(2,128)}, u32[]{:S(2)}) copy-start(f32[256,2]{0,1:T(2,128)} %copy-done.34) | copy-start | bytes 6148
  415.2 27.3 %copy-start.45 = (f32[256]{0:T(256)S(1)}, f32[256]{0:T(256)}, u32[]{:S(2)}) copy-start(f32[256]{0:T(256)} %copy-done.43) | copy-start | bytes 3076
  416.5 207.2 %reduce-scatter.22.cloned.1.call-start = ((), (), s32[]{:S(2)}) async-start(), calls=%async_computation.20 | async-start | bytes 540672 | tf_op jit(solution)/shard_map/reduce_scatter | solution.py:306
  417.8 285.6 %reduce-scatter.18.cloned.1.call-start = ((), (), s32[]{:S(2)}) async-start(), calls=%async_computation.18 | async-start | bytes 270336 | tf_op jit(solution)/shard_map/reduce_scatter | solution.py:300
  443.7 339.3 %reduce-scatter.20.cloned.1.call-start = ((), (), s32[]{:S(2)}) async-start(), calls=%async_computation.19 | async-start | bytes 270336 | tf_op jit(solution)/shard_map/reduce_scatter | solution.py:303
  444.9 420.2 %reduce-scatter.28.cloned.1.call-start = ((), (), s32[]{:S(2)}) async-start(), calls=%async_computation.24 | async-start | bytes 2433024
  452.6 495.1 %reduce-scatter.24.cloned.1.call-start = ((), (), s32[]{:S(2)}) async-start(), calls=%async_computation.21 | async-start | bytes 2433024 | tf_op jit(solution)/shard_map/reduce_scatter | solution.py:309
  456.0 573.8 %reduce-scatter.26.cloned.1.call-start = ((), (), s32[]{:S(2)}) async-start(), calls=%async_computation.22 | async-start | bytes 2433024 | tf_op jit(solution)/shard_map/reduce_scatter | solution.py:312
  458.7 603.0 %all-gather.15.cloned.1.call-start = ((), (), s32[]{:S(2)}) async-start(), calls=%async_computation.23 | async-start | bytes 2621440 | tf_op jit(solution)/shard_map/all_gather | solution.py:271
  460.0 165.0 %copy-start.54 = (f32[64]{0:T(128)S(1)}, f32[64]{0:T(128)}, u32[]{:S(2)}) copy-start(f32[64]{0:T(128)} %get-tuple-element.147) | copy-start | bytes 772
  (40 other events, 135.0 us)
Sparse Core Ops, SparseCore 0:
  141.2 22.5 all-gather.6
  200.5 42.4 all-reduce.13
  345.9 42.2 all-reduce.15
  408.5 32.7 reduce-scatter.13
  443.5 20.0 reduce-scatter.11
  466.9 76.8 reduce-scatter.15
  547.3 76.3 reduce-scatter.21
  627.1 76.2 reduce-scatter.17
  706.8 76.2 reduce-scatter.19
  786.4 78.6 reduce-scatter.27
  869.1 78.5 reduce-scatter.23
  951.2 78.5 reduce-scatter.25
  1031.6 30.1 all-gather.14
Sparse Core Ops, SparseCore 1:
  203.1 43.0 all-gather.8
  248.2 43.6 all-gather.10
  294.0 43.6 all-gather.12
